TPU v7x, 256 devices: a whole 4x4x8 slice. The times are simulated.
256 devices in a mesh: fx: 32 (over z, x), fy: 8 (over y, core).
Axes of the slice: x: 4, y: 4, z: 8, core: 2. Of those that a mesh axis runs over, the one named last changes fastest.
Arguments:
- right_side: float32 [4096, 2048], P(('fx', 'fy'))
- coupling: float32 [4096, 11, 4096], P(('fx', 'fy')), may hold values from -0.109375 to 0.109375
- face_columns: int32 [4096, 11], P(('fx', 'fy')), may hold values from 0 to 31, as said below
- ghost_lists: int32 [1024, 4], P(('fx', 'fy')), may hold values from 0 to 15, as said below
Outputs:
- solution: float32 [4096, 2048], P(('fx', 'fy'))
- residual: float32 [4096, 2048], P(('fx', 'fy'))
Inputs may be any that keep to these rules, and one draw needn't show every extreme that they name: face_columns[f, 0] is f's own index within its block; entries 1 to 6 name other faces of the same block, all distinct and below 16; entries 7 to 10 are distinct and name received faces, 16 + d * 4 + g for the g-th face of group d of the extended list; every received slot of every block is named by some row of that block. `ghost_lists`: each row names 4 distinct faces of its block by local index.
All inputs are finite; a program needn't handle non-finite values.
Results may differ from a plain program's by a relative error of at most 0.0003.
Values sent between devices are 32-bit elements; how exact they have to be, the bound alone decides.
No kernel may reach another device: no remote copies, remote signals or barrier semaphores. Data moves between devices by JAX's collectives and lax.ppermute only.
A program may use at most 64 MiB of HBM per device.

v0:
```python
import jax
import jax.numpy as jnp
from jax import lax
from jax.sharding import PartitionSpec as P

DOF = 64
NRHS = 32
BLOCKS = 11
POWERS = 3


def from_behind(block, axis, distance):
    devices = range(lax.axis_size(axis))
    route = [(i - distance, i) for i in devices if i - distance in devices]
    return lax.ppermute(block, axis, route)


def receive_rows(field, ghost_lists):
    from_lower_x = from_behind(jnp.take(field, ghost_lists[1], axis=0), "fx", 1)
    from_upper_x = from_behind(jnp.take(field, ghost_lists[0], axis=0), "fx", -1)
    from_lower_y = from_behind(jnp.take(field, ghost_lists[3], axis=0), "fy", 1)
    from_upper_y = from_behind(jnp.take(field, ghost_lists[2], axis=0), "fy", -1)
    return jnp.concatenate([from_lower_x, from_upper_x, from_lower_y, from_upper_y], axis=0)


def contract(block_mats, picked):
    face_count = picked.shape[0]
    shaped = picked.reshape(face_count, picked.shape[1], DOF, NRHS)
    result = jnp.einsum("fkab,fkbr->far", block_mats, shaped, precision=lax.Precision.HIGHEST)
    return result.reshape(face_count, DOF * NRHS)


def solve_small(gram_total):
    count = NRHS
    row_ids = jnp.arange((POWERS + 1) * count)[:, None]
    col_ids = jnp.arange(POWERS * count)[None, :]
    shift_map = ((row_ids == col_ids) | (row_ids == col_ids + count)).astype(jnp.float32)
    first = (row_ids == jnp.arange(count)[None, :]).astype(jnp.float32)
    high = lax.Precision.HIGHEST
    normal_matrix = jnp.dot(
        shift_map.T, jnp.dot(gram_total, shift_map, precision=high), precision=high
    )
    right_terms = jnp.dot(shift_map.T, gram_total[:, :count], precision=high)
    factor = jnp.linalg.cholesky(normal_matrix)
    coeffs = jax.scipy.linalg.cho_solve((factor, True), right_terms)
    combo = first - jnp.dot(shift_map, coeffs, precision=high)
    return (coeffs, combo)


def on_device(right_side, coupling, face_columns, ghost_lists):
    face_count = right_side.shape[0]
    block_mats = coupling.reshape(face_count, BLOCKS, DOF, DOF)
    high = lax.Precision.HIGHEST

    def as_rows(field):
        return field.reshape(face_count * DOF, NRHS)

    fields = [right_side]
    for power_index in range(POWERS):
        power_field = fields[-1]
        received = receive_rows(power_field, ghost_lists)
        extended = jnp.concatenate([power_field, received], axis=0)
        fields.append(contract(block_mats, jnp.take(extended, face_columns, axis=0)))
    stacked = jnp.concatenate([as_rows(item) for item in fields], axis=1)
    local_gram = jnp.dot(stacked.T, stacked, precision=high, preferred_element_type=jnp.float32)
    gram_total = lax.psum(local_gram, ("fx", "fy"))
    coeffs, combo = solve_small(gram_total)
    solution = jnp.dot(stacked[:, : POWERS * NRHS], coeffs, precision=high)
    residual = jnp.dot(stacked, combo, precision=high)
    return (solution.reshape(face_count, DOF * NRHS), residual.reshape(face_count, DOF * NRHS))


def solution(mesh):
    placed = (
        P(("fx", "fy"), None),
        P(("fx", "fy"), None, None),
        P(("fx", "fy"), None),
        P(("fx", "fy"), None),
    )
    return jax.shard_map(
        on_device,
        mesh=mesh,
        in_specs=placed,
        out_specs=(P(("fx", "fy"), None), P(("fx", "fy"), None)),
        check_vma=False,
    )
```

profile of v0, /device:TPU:1, one launch (start us, length us, event | category | flops | bytes accessed | tf_op | source)
XLA Modules:
  0.0 415.1 jit_solution(4617153673329050650)
XLA Ops:
  7.2 0.8 compare_and_fusion.1
  8.1 1.5 gather_fusion
  9.6 3.9 collective-permute-start
  13.6 1.5 gather_fusion.1
  15.2 1.3 collective-permute-start.1
  16.5 1.5 gather_fusion.2
  18.0 4.0 collective-permute-start.2
  22.1 1.5 gather_fusion.3
  23.7 1.9 collective-permute-start.3
  25.6 0.7 compare_select_fusion
  26.3 0.7 compare_and_fusion
  27.1 5.7 %reshape.61 = f32[16,11,64,64]{3,2,0,1:T(8,128)} reshape(f32[16,11,4096]{2,0,1:T(8,128)} %param.9) | data formatting | bytes 5767168 | tf_op jit(solution)/shard_map/reshape | solution.py:52
  32.9 1.2 gather_fusion.4
  34.1 1.5 reshape.217
  35.6 1.8 broadcast_select_fusion.2
  37.4 3.6 reshape.245
  41.0 12.0 %fusion.6 = f32[16,64,32]{1,2,0:T(8,128)S(1)} fusion(f32[16,11,64,64]{3,2,0,1:T(8,128)} %reshape.61, f32[16,11,64,32]{3,2,1,0:T(8,128)} %reshape.245), kind=kOutput, calls=%fused_computation.21 | convolution fusion | flops 276824064 | bytes 4456448 | tf_op jit(solution)/shard_map/fkab,fkbr->far/dot_general | solution.py:29
  53.0 0.2 copy.50
  53.2 0.2 reshape.62
  53.4 0.6 gather_fusion.6
  54.0 0.6 gather_fusion.7
  54.6 0.6 gather_fusion.8
  55.2 0.6 gather_fusion.5
  55.8 1.3 collective-permute-start.5
  57.2 3.6 collective-permute-start.6
  60.9 1.9 collective-permute-start.7
  62.9 5.1 %collective-permute-start.4 = (f32[4,2048]{1,0:T(4,128)S(1)}, f32[4,2048]{1,0:T(4,128)S(1)}, u32[]{:S(2)}, u32[]{:S(2)}) collective-permute-start(f32[4,2048]{1,0:T(4,128)S(1)} %broadcast_select_fusion.10), channel_id=1, source_target_pairs={{0,8},{8,16},{16,24},{24,32},{32,40},{40,48},{48,56},{56,64},{64,7... | collective-permute-start | bytes 98312 | tf_op jit(solution)/shard_map/ppermute | solution.py:15
  68.0 0.8 collective-permute-done.4
  68.9 1.2 gather_fusion.9
  70.0 1.6 reshape.229
  71.7 3.2 broadcast_select_fusion.1
  74.9 5.2 %reshape.246 = f32[16,11,64,32]{3,2,1,0:T(8,128)} reshape(f32[16,11,2048]{2,1,0:T(8,128)} %broadcast_select_fusion.1) | data formatting | bytes 2883584 | tf_op jit(solution)/shard_map/reshape | solution.py:28
  80.1 12.0 %fusion.9 = f32[16,64,32]{1,2,0:T(8,128)S(1)} fusion(f32[16,11,64,64]{3,2,0,1:T(8,128)} %reshape.61, f32[16,11,64,32]{3,2,1,0:T(8,128)} %reshape.246), kind=kOutput, calls=%fused_computation.22 | convolution fusion | flops 276824064 | bytes 4456448 | tf_op jit(solution)/shard_map/fkab,fkbr->far/dot_general | solution.py:29
  92.3 0.2 reshape.64
  92.6 0.6 gather_fusion.12
  93.1 0.6 gather_fusion.13
  93.7 0.6 gather_fusion.11
  94.3 0.6 gather_fusion.10
  94.9 4.5 %collective-permute-start.10 = (f32[4,2048]{1,0:T(4,128)S(1)}, f32[4,2048]{1,0:T(4,128)S(1)}, u32[]{:S(2)}, u32[]{:S(2)}) collective-permute-start(f32[4,2048]{1,0:T(4,128)S(1)} %broadcast_select_fusion.4), channel_id=1, source_target_pairs={{0,1},{1,2},{2,3},{3,4},{4,5},{5,6},{6,7},{8,9},{9,10},{10,11},{11... | collective-permute-start | bytes 98312 | tf_op jit(solution)/shard_map/ppermute | solution.py:15
  99.5 1.9 collective-permute-start.11
  101.5 1.3 collective-permute-start.9
  102.9 4.8 %collective-permute-start.8 = (f32[4,2048]{1,0:T(4,128)S(1)}, f32[4,2048]{1,0:T(4,128)S(1)}, u32[]{:S(2)}, u32[]{:S(2)}) collective-permute-start(f32[4,2048]{1,0:T(4,128)S(1)} %broadcast_select_fusion.6), channel_id=1, source_target_pairs={{0,8},{8,16},{16,24},{24,32},{32,40},{40,48},{48,56},{56,64},{64,7... | collective-permute-start | bytes 98312 | tf_op jit(solution)/shard_map/ppermute | solution.py:15
  107.9 0.6 collective-permute-done.8
  108.5 1.2 gather_fusion.14
  109.7 1.6 reshape.241
  111.3 3.2 broadcast_select_fusion
  114.6 5.2 %reshape.247 = f32[16,11,64,32]{3,2,1,0:T(8,128)} reshape(f32[16,11,2048]{2,1,0:T(8,128)} %broadcast_select_fusion) | data formatting | bytes 2883584 | tf_op jit(solution)/shard_map/reshape | solution.py:28
  119.7 12.3 %fusion.12 = f32[16,64,32]{1,2,0:T(8,128)S(1)} fusion(f32[16,11,64,64]{3,2,0,1:T(8,128)} %reshape.61, f32[16,11,64,32]{3,2,1,0:T(8,128)} %reshape.247), kind=kOutput, calls=%fused_computation.23 | convolution fusion | flops 276824064 | bytes 4456448 | tf_op jit(solution)/shard_map/fkab,fkbr->far/dot_general | solution.py:29
  132.2 0.5 pad_maximum_fusion
  132.7 1.6 fusion.37
  134.4 250.2 %all-reduce.2.cloned.1.call-done = f32[128,128]{1,0:T(8,128)} async-done(((f32[128,128]{1,0:T(8,128)}), f32[128,128]{1,0:T(8,128)}) %all-reduce.2.cloned.1.call-update) | async-done | bytes 65552 | tf_op jit(solution)/shard_map/psum | solution.py:66
  384.6 1.0 fusion.34
  385.6 0.2 fusion.32
  385.9 8.8 %cholesky.16 = f32[96,96]{1,0:T(8,128)S(1)} custom-call(f32[96,96]{1,0:T(8,128)S(1)} %fusion.29), custom_call_target="Cholesky" | custom-call | tf_op jit(solution)/shard_map/jit(cholesky)/cholesky | solution.py:44
  394.8 0.6 compare_reduce_fusion
  395.4 0.7 fusion.24
  396.1 7.4 %custom-call.10 = f32[1,96,96]{1,2,0:T(8,128)S(1)} custom-call(f32[1,96,96]{2,1,0:T(8,128)S(1)} %fusion.24), custom_call_target="InvertDiagBlocksLowerTriangular" | custom-call | tf_op jit(solution)/shard_map/jit(_cho_solve)/triangular_solve | solution.py:45
  403.4 1.1 fusion.21
  404.5 0.3 fusion.27
  404.8 0.2 fusion.25
  405.2 0.7 fusion.15
  405.9 0.6 fusion.38
  406.5 0.9 reshape.67
  407.4 0.9 reshape.66
  (43 shorter events, 2.3 us)
Async XLA Ops:
  7.2 377.4 %all-reduce.2.cloned.1.call-start = ((), (), s32[]{:S(2)}) async-start(), calls=%async_computation | async-start | bytes 131072 | tf_op jit(solution)/shard_map/psum | solution.py:66
  9.6 23.2 %collective-permute-start = (f32[4,2048]{1,0:T(4,128)S(1)}, f32[4,2048]{1,0:T(4,128)S(1)}, u32[]{:S(2)}, u32[]{:S(2)}) collective-permute-start(f32[4,2048]{1,0:T(4,128)S(1)} %broadcast_select_fusion.14), channel_id=1, source_target_pairs={{0,8},{8,16},{16,24},{24,32},{32,40},{40,48},{48,56},{56,64},{64,7... | collective-permute-start | bytes 98312 | tf_op jit(solution)/shard_map/ppermute | solution.py:15
  15.2 17.6 %collective-permute-start.1 = (f32[4,2048]{1,0:T(4,128)S(1)}, f32[4,2048]{1,0:T(4,128)S(1)}, u32[]{:S(2)}, u32[]{:S(2)}) collective-permute-start(f32[4,2048]{1,0:T(4,128)S(1)} %broadcast_select_fusion.13), channel_id=1, source_target_pairs={{8,0},{16,8},{24,16},{32,24},{40,32},{48,40},{56,48},{64,56},{72,6... | collective-permute-start | bytes 98312 | tf_op jit(solution)/shard_map/ppermute | solution.py:15
  18.0 14.8 %collective-permute-start.2 = (f32[4,2048]{1,0:T(4,128)S(1)}, f32[4,2048]{1,0:T(4,128)S(1)}, u32[]{:S(2)}, u32[]{:S(2)}) collective-permute-start(f32[4,2048]{1,0:T(4,128)S(1)} %broadcast_select_fusion.12), channel_id=1, source_target_pairs={{0,1},{1,2},{2,3},{3,4},{4,5},{5,6},{6,7},{8,9},{9,10},{10,11},{11... | collective-permute-start | bytes 98312 | tf_op jit(solution)/shard_map/ppermute | solution.py:15
  23.7 9.2 %collective-permute-start.3 = (f32[4,2048]{1,0:T(4,128)S(1)}, f32[4,2048]{1,0:T(4,128)S(1)}, u32[]{:S(2)}, u32[]{:S(2)}) collective-permute-start(f32[4,2048]{1,0:T(4,128)S(1)} %broadcast_select_fusion.11), channel_id=1, source_target_pairs={{1,0},{2,1},{3,2},{4,3},{5,4},{6,5},{7,6},{9,8},{10,9},{11,10},{12... | collective-permute-start | bytes 98312 | tf_op jit(solution)/shard_map/ppermute | solution.py:15
  27.1 5.7 %copy-start = (f32[16,2048]{1,0:T(8,128)S(1)}, f32[16,2048]{1,0:T(8,128)}, u32[]{:S(2)}) copy-start(f32[16,2048]{1,0:T(8,128)} %param.8) | copy-start | bytes 393220
  55.8 12.2 %collective-permute-start.5 = (f32[4,2048]{1,0:T(4,128)S(1)}, f32[4,2048]{1,0:T(4,128)S(1)}, u32[]{:S(2)}, u32[]{:S(2)}) collective-permute-start(f32[4,2048]{1,0:T(4,128)S(1)} %broadcast_select_fusion.9), channel_id=1, source_target_pairs={{8,0},{16,8},{24,16},{32,24},{40,32},{48,40},{56,48},{64,56},{72,6... | collective-permute-start | bytes 98312 | tf_op jit(solution)/shard_map/ppermute | solution.py:15
  57.2 10.8 %collective-permute-start.6 = (f32[4,2048]{1,0:T(4,128)S(1)}, f32[4,2048]{1,0:T(4,128)S(1)}, u32[]{:S(2)}, u32[]{:S(2)}) collective-permute-start(f32[4,2048]{1,0:T(4,128)S(1)} %broadcast_select_fusion.8), channel_id=1, source_target_pairs={{0,1},{1,2},{2,3},{3,4},{4,5},{5,6},{6,7},{8,9},{9,10},{10,11},{11... | collective-permute-start | bytes 98312 | tf_op jit(solution)/shard_map/ppermute | solution.py:15
  60.9 7.1 %collective-permute-start.7 = (f32[4,2048]{1,0:T(4,128)S(1)}, f32[4,2048]{1,0:T(4,128)S(1)}, u32[]{:S(2)}, u32[]{:S(2)}) collective-permute-start(f32[4,2048]{1,0:T(4,128)S(1)} %broadcast_select_fusion.7), channel_id=1, source_target_pairs={{1,0},{2,1},{3,2},{4,3},{5,4},{6,5},{7,6},{9,8},{10,9},{11,10},{12... | collective-permute-start | bytes 98312 | tf_op jit(solution)/shard_map/ppermute | solution.py:15
  62.9 5.9 %collective-permute-start.4 = (f32[4,2048]{1,0:T(4,128)S(1)}, f32[4,2048]{1,0:T(4,128)S(1)}, u32[]{:S(2)}, u32[]{:S(2)}) collective-permute-start(f32[4,2048]{1,0:T(4,128)S(1)} %broadcast_select_fusion.10), channel_id=1, source_target_pairs={{0,8},{8,16},{16,24},{24,32},{32,40},{40,48},{48,56},{56,64},{64,7... | collective-permute-start | bytes 98312 | tf_op jit(solution)/shard_map/ppermute | solution.py:15
  94.9 12.9 %collective-permute-start.10 = (f32[4,2048]{1,0:T(4,128)S(1)}, f32[4,2048]{1,0:T(4,128)S(1)}, u32[]{:S(2)}, u32[]{:S(2)}) collective-permute-start(f32[4,2048]{1,0:T(4,128)S(1)} %broadcast_select_fusion.4), channel_id=1, source_target_pairs={{0,1},{1,2},{2,3},{3,4},{4,5},{5,6},{6,7},{8,9},{9,10},{10,11},{11... | collective-permute-start | bytes 98312 | tf_op jit(solution)/shard_map/ppermute | solution.py:15
  99.5 8.3 %collective-permute-start.11 = (f32[4,2048]{1,0:T(4,128)S(1)}, f32[4,2048]{1,0:T(4,128)S(1)}, u32[]{:S(2)}, u32[]{:S(2)}) collective-permute-start(f32[4,2048]{1,0:T(4,128)S(1)} %broadcast_select_fusion.3), channel_id=1, source_target_pairs={{1,0},{2,1},{3,2},{4,3},{5,4},{6,5},{7,6},{9,8},{10,9},{11,10},{12... | collective-permute-start | bytes 98312 | tf_op jit(solution)/shard_map/ppermute | solution.py:15
  101.5 6.3 %collective-permute-start.9 = (f32[4,2048]{1,0:T(4,128)S(1)}, f32[4,2048]{1,0:T(4,128)S(1)}, u32[]{:S(2)}, u32[]{:S(2)}) collective-permute-start(f32[4,2048]{1,0:T(4,128)S(1)} %broadcast_select_fusion.5), channel_id=1, source_target_pairs={{8,0},{16,8},{24,16},{32,24},{40,32},{48,40},{56,48},{64,56},{72,6... | collective-permute-start | bytes 98312 | tf_op jit(solution)/shard_map/ppermute | solution.py:15
  102.9 5.6 %collective-permute-start.8 = (f32[4,2048]{1,0:T(4,128)S(1)}, f32[4,2048]{1,0:T(4,128)S(1)}, u32[]{:S(2)}, u32[]{:S(2)}) collective-permute-start(f32[4,2048]{1,0:T(4,128)S(1)} %broadcast_select_fusion.6), channel_id=1, source_target_pairs={{0,8},{8,16},{16,24},{24,32},{32,40},{40,48},{48,56},{56,64},{64,7... | collective-permute-start | bytes 98312 | tf_op jit(solution)/shard_map/ppermute | solution.py:15
Sparse Core Ops, SparseCore 0:
  134.5 250.0 all-reduce.1
where the time goes:
time: 416 us; the launch traced here: 415 us
  waiting for transfers between devices  252 us (61%)
  matrix products  42.2 us (10%)
  local copies, waits for them, and re-layouts  41.9 us (10%)
  starting transfers between devices  35.5 us (9%)
  other arithmetic  29.4 us (7%)
  between operations  14.5 us (3%)
    psum x1, waiting for transfers between devices, on_device(): gram_total = lax.psum(local_gram, ('fx', 'fy'))  250 us
    dot_general x3, matrix products, contract(): jnp.einsum('fkab,fkbr->far', block_mats, shaped, precision=lax.Precision....  36.3 us
    ppermute x12, starting transfers between devices, from_behind(): return lax.ppermute(block, axis, route)  35.5 us
    reshape x3, local copies, waits for them, and re-layouts, contract(): shaped = picked.reshape(face_count, picked.shape[1], DOF, NRHS)  13.9 us
    another operation x3, other arithmetic, solve_small(): factor = jnp.linalg.cholesky(normal_matrix)  9.45 us
    select_n x4, other arithmetic, on_device(): jnp.take(extended, face_columns, axis=0)  8.94 us
  transfers between devices with their start and end apart: 13, of which 3 were waited for; matrix products, arithmetic and copies ran while one was open for 3% of the time, Pallas kernels for 0%

commit v1 on v0

--- a/solution.py
+++ b/solution.py
@@ -63,7 +63,8 @@
         fields.append(contract(block_mats, jnp.take(extended, face_columns, axis=0)))
     stacked = jnp.concatenate([as_rows(item) for item in fields], axis=1)
     local_gram = jnp.dot(stacked.T, stacked, precision=high, preferred_element_type=jnp.float32)
-    gram_total = lax.psum(local_gram, ("fx", "fy"))
+    half = lax.psum(local_gram, "fx")
+    gram_total = lax.psum(half, "fy")
     coeffs, combo = solve_small(gram_total)
     solution = jnp.dot(stacked[:, : POWERS * NRHS], coeffs, precision=high)
     residual = jnp.dot(stacked, combo, precision=high)

time: 416 us -> 381 us (0.916)
  waiting for transfers between devices: 252 us -> 215 us
    psum x1 -> x2, waiting for transfers between devices: 250 us -> 213 us  [the longest x1 147 us: on_device(): half = lax.psum(local_gram, 'fx')]
  transfers between devices with their start and end apart: 13 -> 14, of which waited for: 3 -> 4; matrix products, arithmetic and copies ran while one was open for 3% -> 3% of each run, Pallas kernels for 0% -> 0%
where the time goes in v1:
time: 381 us; the launch traced here: 378 us
  waiting for transfers between devices  215 us (56%)
  matrix products  42 us (11%)
  local copies, waits for them, and re-layouts  41.9 us (11%)
  starting transfers between devices  35.8 us (9%)
  other arithmetic  29.4 us (8%)
  between operations  14.5 us (4%)
    psum x1, waiting for transfers between devices, on_device(): half = lax.psum(local_gram, 'fx')  147 us
    psum x1, waiting for transfers between devices, on_device(): gram_total = lax.psum(half, 'fy')  66.4 us
    dot_general x3, matrix products, contract(): jnp.einsum('fkab,fkbr->far', block_mats, shaped, precision=lax.Precision....  36 us
    ppermute x12, starting transfers between devices, from_behind(): return lax.ppermute(block, axis, route)  35.5 us
    reshape x3, local copies, waits for them, and re-layouts, contract(): shaped = picked.reshape(face_count, picked.shape[1], DOF, NRHS)  13.9 us
    another operation x3, other arithmetic, solve_small(): factor = jnp.linalg.cholesky(normal_matrix)  9.45 us
    select_n x4, other arithmetic, on_device(): jnp.take(extended, face_columns, axis=0)  8.94 us
    gather x6, local copies, waits for them, and re-layouts, on_device(): jnp.take(extended, face_columns, axis=0)  8.28 us
  transfers between devices with their start and end apart: 14, of which 4 were waited for; matrix products, arithmetic and copies ran while one was open for 3% of the time, Pallas kernels for 0%

profile of v1, /device:TPU:1, one launch (start us, length us, event | category | flops | bytes accessed | tf_op | source)
XLA Modules:
  0.0 378.3 jit_solution(7321667405650239549)
XLA Ops:
  7.2 0.8 compare_and_fusion.1
  8.1 1.5 gather_fusion
  9.6 3.9 %collective-permute-start = (f32[4,2048]{1,0:T(4,128)S(1)}, f32[4,2048]{1,0:T(4,128)S(1)}, u32[]{:S(2)}, u32[]{:S(2)}) collective-permute-start(f32[4,2048]{1,0:T(4,128)S(1)} %broadcast_select_fusion.14), channel_id=1, source_target_pairs={{0,8},{8,16},{16,24},{24,32},{32,40},{40,48},{48,56},{56,64},{64,7... | collective-permute-start | bytes 98312 | tf_op jit(solution)/shard_map/ppermute | solution.py:15
  13.6 1.5 gather_fusion.1
  15.2 1.3 collective-permute-start.1
  16.5 1.5 gather_fusion.2
  18.0 4.0 %collective-permute-start.2 = (f32[4,2048]{1,0:T(4,128)S(1)}, f32[4,2048]{1,0:T(4,128)S(1)}, u32[]{:S(2)}, u32[]{:S(2)}) collective-permute-start(f32[4,2048]{1,0:T(4,128)S(1)} %broadcast_select_fusion.12), channel_id=1, source_target_pairs={{0,1},{1,2},{2,3},{3,4},{4,5},{5,6},{6,7},{8,9},{9,10},{10,11},{11... | collective-permute-start | bytes 98312 | tf_op jit(solution)/shard_map/ppermute | solution.py:15
  22.1 1.5 gather_fusion.3
  23.7 1.9 collective-permute-start.3
  25.6 0.7 compare_select_fusion
  26.3 0.7 compare_and_fusion
  27.1 5.7 %reshape.61 = f32[16,11,64,64]{3,2,0,1:T(8,128)} reshape(f32[16,11,4096]{2,0,1:T(8,128)} %param.9) | data formatting | bytes 5767168 | tf_op jit(solution)/shard_map/reshape | solution.py:52
  32.9 1.2 gather_fusion.4
  34.1 1.5 reshape.217
  35.6 1.8 broadcast_select_fusion.2
  37.4 3.6 reshape.245
  41.0 12.0 %fusion.6 = f32[16,64,32]{1,2,0:T(8,128)S(1)} fusion(f32[16,11,64,64]{3,2,0,1:T(8,128)} %reshape.61, f32[16,11,64,32]{3,2,1,0:T(8,128)} %reshape.245), kind=kOutput, calls=%fused_computation.21 | convolution fusion | flops 276824064 | bytes 4456448 | tf_op jit(solution)/shard_map/fkab,fkbr->far/dot_general | solution.py:29
  53.2 0.2 reshape.62
  53.4 0.6 gather_fusion.6
  54.0 0.6 gather_fusion.7
  54.6 0.6 gather_fusion.8
  55.2 0.6 gather_fusion.5
  55.8 1.3 collective-permute-start.5
  57.2 3.6 collective-permute-start.6
  60.9 1.9 collective-permute-start.7
  62.9 5.1 %collective-permute-start.4 = (f32[4,2048]{1,0:T(4,128)S(1)}, f32[4,2048]{1,0:T(4,128)S(1)}, u32[]{:S(2)}, u32[]{:S(2)}) collective-permute-start(f32[4,2048]{1,0:T(4,128)S(1)} %broadcast_select_fusion.10), channel_id=1, source_target_pairs={{0,8},{8,16},{16,24},{24,32},{32,40},{40,48},{48,56},{56,64},{64,7... | collective-permute-start | bytes 98312 | tf_op jit(solution)/shard_map/ppermute | solution.py:15
  68.0 0.8 collective-permute-done.4
  68.9 1.2 gather_fusion.9
  70.0 1.6 reshape.229
  71.7 3.2 broadcast_select_fusion.1
  74.9 5.2 %reshape.246 = f32[16,11,64,32]{3,2,1,0:T(8,128)} reshape(f32[16,11,2048]{2,1,0:T(8,128)} %broadcast_select_fusion.1) | data formatting | bytes 2883584 | tf_op jit(solution)/shard_map/reshape | solution.py:28
  80.1 12.0 %fusion.9 = f32[16,64,32]{1,2,0:T(8,128)S(1)} fusion(f32[16,11,64,64]{3,2,0,1:T(8,128)} %reshape.61, f32[16,11,64,32]{3,2,1,0:T(8,128)} %reshape.246), kind=kOutput, calls=%fused_computation.22 | convolution fusion | flops 276824064 | bytes 4456448 | tf_op jit(solution)/shard_map/fkab,fkbr->far/dot_general | solution.py:29
  92.3 0.2 reshape.64
  92.6 0.6 gather_fusion.12
  93.1 0.6 gather_fusion.13
  93.7 0.6 gather_fusion.11
  94.3 0.6 gather_fusion.10
  94.9 4.5 %collective-permute-start.10 = (f32[4,2048]{1,0:T(4,128)S(1)}, f32[4,2048]{1,0:T(4,128)S(1)}, u32[]{:S(2)}, u32[]{:S(2)}) collective-permute-start(f32[4,2048]{1,0:T(4,128)S(1)} %broadcast_select_fusion.4), channel_id=1, source_target_pairs={{0,1},{1,2},{2,3},{3,4},{4,5},{5,6},{6,7},{8,9},{9,10},{10,11},{11... | collective-permute-start | bytes 98312 | tf_op jit(solution)/shard_map/ppermute | solution.py:15
  99.5 1.9 collective-permute-start.11
  101.5 1.3 collective-permute-start.9
  102.9 4.8 %collective-permute-start.8 = (f32[4,2048]{1,0:T(4,128)S(1)}, f32[4,2048]{1,0:T(4,128)S(1)}, u32[]{:S(2)}, u32[]{:S(2)}) collective-permute-start(f32[4,2048]{1,0:T(4,128)S(1)} %broadcast_select_fusion.6), channel_id=1, source_target_pairs={{0,8},{8,16},{16,24},{24,32},{32,40},{40,48},{48,56},{56,64},{64,7... | collective-permute-start | bytes 98312 | tf_op jit(solution)/shard_map/ppermute | solution.py:15
  107.9 0.6 collective-permute-done.8
  108.5 1.2 gather_fusion.14
  109.7 1.6 reshape.241
  111.3 3.2 broadcast_select_fusion
  114.6 5.2 %reshape.247 = f32[16,11,64,32]{3,2,1,0:T(8,128)} reshape(f32[16,11,2048]{2,1,0:T(8,128)} %broadcast_select_fusion) | data formatting | bytes 2883584 | tf_op jit(solution)/shard_map/reshape | solution.py:28
  119.7 12.0 %fusion.12 = f32[16,64,32]{1,2,0:T(8,128)S(1)} fusion(f32[16,11,64,64]{3,2,0,1:T(8,128)} %reshape.61, f32[16,11,64,32]{3,2,1,0:T(8,128)} %reshape.247), kind=kOutput, calls=%fused_computation.23 | convolution fusion | flops 276824064 | bytes 4456448 | tf_op jit(solution)/shard_map/fkab,fkbr->far/dot_general | solution.py:29
  132.0 0.5 pad_maximum_fusion
  132.4 1.6 fusion.37
  134.1 0.3 all-reduce.5.cloned.1.call-start
  134.4 146.8 %all-reduce.3.cloned.1.call-done = f32[128,128]{1,0:T(8,128)} async-done(((f32[128,128]{1,0:T(8,128)}), f32[128,128]{1,0:T(8,128)}) %all-reduce.3.cloned.1.call-update) | async-done | bytes 65552 | tf_op jit(solution)/shard_map/psum | solution.py:66
  281.3 66.4 %all-reduce.5.cloned.1.call-done = f32[128,128]{1,0:T(8,128)} async-done(((f32[128,128]{1,0:T(8,128)}), f32[128,128]{1,0:T(8,128)}) %all-reduce.5.cloned.1.call-update) | async-done | bytes 65552 | tf_op jit(solution)/shard_map/psum | solution.py:67
  347.7 1.0 fusion.34
  348.7 0.2 fusion.32
  349.1 8.8 %cholesky.16 = f32[96,96]{1,0:T(8,128)S(1)} custom-call(f32[96,96]{1,0:T(8,128)S(1)} %fusion.29), custom_call_target="Cholesky" | custom-call | tf_op jit(solution)/shard_map/jit(cholesky)/cholesky | solution.py:44
  357.9 0.6 compare_reduce_fusion
  358.5 0.7 fusion.24
  359.2 7.4 %custom-call.10 = f32[1,96,96]{1,2,0:T(8,128)S(1)} custom-call(f32[1,96,96]{2,1,0:T(8,128)S(1)} %fusion.24), custom_call_target="InvertDiagBlocksLowerTriangular" | custom-call | tf_op jit(solution)/shard_map/jit(_cho_solve)/triangular_solve | solution.py:45
  366.6 1.1 fusion.21
  367.7 0.3 fusion.27
  368.3 0.7 fusion.15
  369.1 0.6 fusion.38
  369.7 0.9 reshape.67
  370.5 0.9 reshape.66
  (46 shorter events, 2.7 us)
Async XLA Ops:
  7.2 274.1 %all-reduce.3.cloned.1.call-start = ((), (), s32[]{:S(2)}) async-start(), calls=%async_computation | async-start | bytes 131072 | tf_op jit(solution)/shard_map/psum | solution.py:66
  9.6 23.2 %collective-permute-start = (f32[4,2048]{1,0:T(4,128)S(1)}, f32[4,2048]{1,0:T(4,128)S(1)}, u32[]{:S(2)}, u32[]{:S(2)}) collective-permute-start(f32[4,2048]{1,0:T(4,128)S(1)} %broadcast_select_fusion.14), channel_id=1, source_target_pairs={{0,8},{8,16},{16,24},{24,32},{32,40},{40,48},{48,56},{56,64},{64,7... | collective-permute-start | bytes 98312 | tf_op jit(solution)/shard_map/ppermute | solution.py:15
  15.2 17.6 %collective-permute-start.1 = (f32[4,2048]{1,0:T(4,128)S(1)}, f32[4,2048]{1,0:T(4,128)S(1)}, u32[]{:S(2)}, u32[]{:S(2)}) collective-permute-start(f32[4,2048]{1,0:T(4,128)S(1)} %broadcast_select_fusion.13), channel_id=1, source_target_pairs={{8,0},{16,8},{24,16},{32,24},{40,32},{48,40},{56,48},{64,56},{72,6... | collective-permute-start | bytes 98312 | tf_op jit(solution)/shard_map/ppermute | solution.py:15
  18.0 14.8 %collective-permute-start.2 = (f32[4,2048]{1,0:T(4,128)S(1)}, f32[4,2048]{1,0:T(4,128)S(1)}, u32[]{:S(2)}, u32[]{:S(2)}) collective-permute-start(f32[4,2048]{1,0:T(4,128)S(1)} %broadcast_select_fusion.12), channel_id=1, source_target_pairs={{0,1},{1,2},{2,3},{3,4},{4,5},{5,6},{6,7},{8,9},{9,10},{10,11},{11... | collective-permute-start | bytes 98312 | tf_op jit(solution)/shard_map/ppermute | solution.py:15
  23.7 9.2 %collective-permute-start.3 = (f32[4,2048]{1,0:T(4,128)S(1)}, f32[4,2048]{1,0:T(4,128)S(1)}, u32[]{:S(2)}, u32[]{:S(2)}) collective-permute-start(f32[4,2048]{1,0:T(4,128)S(1)} %broadcast_select_fusion.11), channel_id=1, source_target_pairs={{1,0},{2,1},{3,2},{4,3},{5,4},{6,5},{7,6},{9,8},{10,9},{11,10},{12... | collective-permute-start | bytes 98312 | tf_op jit(solution)/shard_map/ppermute | solution.py:15
  27.1 5.7 %copy-start = (f32[16,2048]{1,0:T(8,128)S(1)}, f32[16,2048]{1,0:T(8,128)}, u32[]{:S(2)}) copy-start(f32[16,2048]{1,0:T(8,128)} %param.8) | copy-start | bytes 393220
  55.8 12.2 %collective-permute-start.5 = (f32[4,2048]{1,0:T(4,128)S(1)}, f32[4,2048]{1,0:T(4,128)S(1)}, u32[]{:S(2)}, u32[]{:S(2)}) collective-permute-start(f32[4,2048]{1,0:T(4,128)S(1)} %broadcast_select_fusion.9), channel_id=1, source_target_pairs={{8,0},{16,8},{24,16},{32,24},{40,32},{48,40},{56,48},{64,56},{72,6... | collective-permute-start | bytes 98312 | tf_op jit(solution)/shard_map/ppermute | solution.py:15
  57.2 10.8 %collective-permute-start.6 = (f32[4,2048]{1,0:T(4,128)S(1)}, f32[4,2048]{1,0:T(4,128)S(1)}, u32[]{:S(2)}, u32[]{:S(2)}) collective-permute-start(f32[4,2048]{1,0:T(4,128)S(1)} %broadcast_select_fusion.8), channel_id=1, source_target_pairs={{0,1},{1,2},{2,3},{3,4},{4,5},{5,6},{6,7},{8,9},{9,10},{10,11},{11... | collective-permute-start | bytes 98312 | tf_op jit(solution)/shard_map/ppermute | solution.py:15
  60.9 7.1 %collective-permute-start.7 = (f32[4,2048]{1,0:T(4,128)S(1)}, f32[4,2048]{1,0:T(4,128)S(1)}, u32[]{:S(2)}, u32[]{:S(2)}) collective-permute-start(f32[4,2048]{1,0:T(4,128)S(1)} %broadcast_select_fusion.7), channel_id=1, source_target_pairs={{1,0},{2,1},{3,2},{4,3},{5,4},{6,5},{7,6},{9,8},{10,9},{11,10},{12... | collective-permute-start | bytes 98312 | tf_op jit(solution)/shard_map/ppermute | solution.py:15
  62.9 5.9 %collective-permute-start.4 = (f32[4,2048]{1,0:T(4,128)S(1)}, f32[4,2048]{1,0:T(4,128)S(1)}, u32[]{:S(2)}, u32[]{:S(2)}) collective-permute-start(f32[4,2048]{1,0:T(4,128)S(1)} %broadcast_select_fusion.10), channel_id=1, source_target_pairs={{0,8},{8,16},{16,24},{24,32},{32,40},{40,48},{48,56},{56,64},{64,7... | collective-permute-start | bytes 98312 | tf_op jit(solution)/shard_map/ppermute | solution.py:15
  94.9 12.9 %collective-permute-start.10 = (f32[4,2048]{1,0:T(4,128)S(1)}, f32[4,2048]{1,0:T(4,128)S(1)}, u32[]{:S(2)}, u32[]{:S(2)}) collective-permute-start(f32[4,2048]{1,0:T(4,128)S(1)} %broadcast_select_fusion.4), channel_id=1, source_target_pairs={{0,1},{1,2},{2,3},{3,4},{4,5},{5,6},{6,7},{8,9},{9,10},{10,11},{11... | collective-permute-start | bytes 98312 | tf_op jit(solution)/shard_map/ppermute | solution.py:15
  99.5 8.3 %collective-permute-start.11 = (f32[4,2048]{1,0:T(4,128)S(1)}, f32[4,2048]{1,0:T(4,128)S(1)}, u32[]{:S(2)}, u32[]{:S(2)}) collective-permute-start(f32[4,2048]{1,0:T(4,128)S(1)} %broadcast_select_fusion.3), channel_id=1, source_target_pairs={{1,0},{2,1},{3,2},{4,3},{5,4},{6,5},{7,6},{9,8},{10,9},{11,10},{12... | collective-permute-start | bytes 98312 | tf_op jit(solution)/shard_map/ppermute | solution.py:15
  101.5 6.3 %collective-permute-start.9 = (f32[4,2048]{1,0:T(4,128)S(1)}, f32[4,2048]{1,0:T(4,128)S(1)}, u32[]{:S(2)}, u32[]{:S(2)}) collective-permute-start(f32[4,2048]{1,0:T(4,128)S(1)} %broadcast_select_fusion.5), channel_id=1, source_target_pairs={{8,0},{16,8},{24,16},{32,24},{40,32},{48,40},{56,48},{64,56},{72,6... | collective-permute-start | bytes 98312 | tf_op jit(solution)/shard_map/ppermute | solution.py:15
  102.9 5.6 %collective-permute-start.8 = (f32[4,2048]{1,0:T(4,128)S(1)}, f32[4,2048]{1,0:T(4,128)S(1)}, u32[]{:S(2)}, u32[]{:S(2)}) collective-permute-start(f32[4,2048]{1,0:T(4,128)S(1)} %broadcast_select_fusion.6), channel_id=1, source_target_pairs={{0,8},{8,16},{16,24},{24,32},{32,40},{40,48},{48,56},{56,64},{64,7... | collective-permute-start | bytes 98312 | tf_op jit(solution)/shard_map/ppermute | solution.py:15
  134.1 213.6 %all-reduce.5.cloned.1.call-start = ((), (), s32[]{:S(2)}) async-start(), calls=%async_computation.1 | async-start | bytes 131072 | tf_op jit(solution)/shard_map/psum | solution.py:67
Sparse Core Ops, SparseCore 0:
  134.2 146.9 all-reduce.2
  283.6 64.0 all-reduce.4
